TPU v7x, 128 devices: a whole 4x4x4 slice. The times are simulated.
128 devices in a mesh: freq: 16 (over x, y), slab: 8 (over z, core).
Axes of the slice: x: 4, y: 4, z: 4, core: 2. Of those that a mesh axis runs over, the one named last changes fastest.
Arguments:
- fine_model: bfloat16 [2048, 2048], P(('freq', 'slab')), may hold values from 0.5 to 2
- resample: bfloat16 [16, 1024, 2048], P('freq', 'slab'), may hold values from -0.125 to 0.125
- lateral: bfloat16 [2048, 2048], replicated, may hold values from -0.0625 to 0.0625
- shift: float32 [16], P('freq'), may hold values from 0.5 to 4
- source: float32 [16, 1024, 2048], P('freq', 'slab'), may hold values from -6 to 6
- receiver: float32 [16, 1024, 2048], P('freq', 'slab'), may hold values from -6 to 6
Outputs:
- image: float32 [2048, 2048], P(('freq', 'slab'))
All inputs are finite; a program needn't handle non-finite values.
Results may differ from a plain program's by a relative error of at most 0.0029.
Values may be sent and summed in bfloat16 or wider, within the bound.
A program may use at most 128 MiB of HBM per device.

v0:
```python
import jax
import jax.numpy as jnp
from jax import lax
from jax.sharding import PartitionSpec as P

SWEEPS = 8


def with_halo(value, sides, width):
    for axis, dim in sides:
        size, length = (lax.axis_size(axis), value.shape[dim])
        up = [(i, (i + 1) % size) for i in range(size - 1)]
        down = [(j, i) for i, j in up]
        last = lax.slice_in_dim(value, length - width, length, axis=dim)
        initial = lax.slice_in_dim(value, 0, width, axis=dim)
        before = lax.ppermute(last, axis, up)
        after = lax.ppermute(initial, axis, down)
        value = jnp.concatenate([before, value, after], axis=dim)
    return value


def shards(fine_model, resample, lateral, shift, source, receiver):
    oper = resample[0]
    columns = oper
    coarse = jnp.dot(
        columns,
        lax.all_gather(fine_model, ("freq", "slab"), axis=0, tiled=True),
        preferred_element_type=jnp.float32,
    )
    diag = 4.0 + shift[0] * coarse * coarse
    src = source[0]
    field = jnp.zeros(src.shape, jnp.float32)
    for sweep in range(SWEEPS):
        padded = with_halo(field, (("slab", 0),), 1)
        beside = padded[2:] + padded[:-2]
        side = jnp.dot(field.astype(jnp.bfloat16), lateral, preferred_element_type=jnp.float32)
        field = (src + 0.5 * beside + side) / diag
    partial_img = (field * receiver[0]).astype(jnp.bfloat16)
    columns = oper
    return lax.psum_scatter(
        lax.dot_general(
            columns, partial_img, (((0,), (0,)), ((), ())), preferred_element_type=jnp.float32
        ),
        ("freq", "slab"),
        scatter_dimension=0,
        tiled=True,
    )


def solution(mesh):
    in_specs = (
        P(("freq", "slab"), None),
        P("freq", "slab", None),
        P(),
        P("freq"),
        P("freq", "slab", None),
        P("freq", "slab", None),
    )
    out_specs = P(("freq", "slab"), None)
    return jax.shard_map(shards, mesh=mesh, in_specs=in_specs, out_specs=out_specs, check_vma=False)
```

profile of v0, /device:TPU:0, one launch (start us, length us, event | category | flops | bytes accessed | tf_op | source)
XLA Modules:
  0.0 849.0 jit_solution(14113085635344979376)
XLA Ops:
  6.5 0.0 copy-start
  6.5 0.0 copy-start.1
  6.5 0.0 all-gather.2.cloned.1.call-start
  6.5 0.7 all-gather.2.cloned.1.call-update
  7.3 0.0 reduce-scatter.4.cloned.1.call-start
  7.3 1.3 collective-permute-start.1
  8.6 1.3 collective-permute-start
  10.6 72.4 %all-gather.2.cloned.1.call-done = bf16[2048,2048]{1,0:T(8,128)(2,1)} async-done(((bf16[16,2048]{1,0:T(8,128)(2,1)}), bf16[2048,2048]{1,0:T(8,128)(2,1)}) %all-gather.2.cloned.1.call-update) | async-done | bytes 8388624 | tf_op jit(solution)/shard_map/all_gather | solution.py:27
  83.0 0.0 slice-start
  83.0 0.0 copy-done
  83.0 0.0 slice-start.1
  83.0 4.8 fusion.5
  87.8 0.0 collective-permute-done.1
  87.8 0.0 collective-permute-done
  87.8 0.0 copy-done.1
  87.8 0.0 slice-done
  87.8 1.0 slice-done.1
  88.8 1.3 fusion.4
  90.2 1.3 collective-permute-start.2
  91.5 3.0 collective-permute-start.3
  94.5 0.0 collective-permute-done.2
  94.5 0.8 collective-permute-done.3
  95.3 1.6 fusion.41
  97.0 1.3 collective-permute-start.4
  98.3 4.0 collective-permute-start.5
  102.3 0.0 collective-permute-done.4
  102.3 0.8 collective-permute-done.5
  103.1 1.6 fusion.36
  104.7 1.3 collective-permute-start.6
  106.0 4.8 collective-permute-start.7
  110.8 0.0 collective-permute-done.6
  110.8 0.8 collective-permute-done.7
  111.6 1.6 fusion.31
  113.2 1.3 collective-permute-start.8
  114.5 4.8 collective-permute-start.9
  119.3 0.0 collective-permute-done.8
  119.3 0.8 collective-permute-done.9
  120.1 1.6 fusion.26
  121.8 1.3 collective-permute-start.10
  123.1 0.0 copy-start.2
  123.1 4.9 collective-permute-start.11
  128.0 0.0 collective-permute-done.10
  128.0 0.8 collective-permute-done.11
  128.8 1.6 fusion.21
  130.4 1.3 collective-permute-start.12
  131.7 5.0 collective-permute-start.13
  136.7 0.0 collective-permute-done.12
  136.7 0.6 collective-permute-done.13
  137.3 0.0 copy-done.2
  137.3 1.6 fusion.16
  139.0 1.3 collective-permute-start.14
  140.3 4.8 collective-permute-start.15
  145.0 0.0 collective-permute-done.14
  145.1 0.8 collective-permute-done.15
  145.9 12.7 %convolution_bitcast_fusion = f32[2048,2048]{0,1:T(8,128)} fusion(f32[1,128,2048]{2,1,0:T(8,128)} %param.11, f32[128,2048]{1,0:T(8,128)S(1)} %fusion.5, f32[128,2048]{1,0:T(8,128)S(1)} %fusion.16, f32[1,2048]{1,0:T(1,128)S(1)} %collective-permute-done.15, f32[1,2048]{1,0:T(1,128)S(1)} %collective-permute-done.14, f32[1,128,2048]{2,1,0:T(8,128)} %param.10, ...), kind=kOutput, calls=%fused_computation | convolution fusion | flops 2150105088 | bytes 29900800 | tf_op jit(solution)/shard_map/dot_general | solution.py:41
  158.5 17.6 %copy.9 = f32[2048,2048]{1,0:T(8,128)} copy(f32[2048,2048]{0,1:T(8,128)} %convolution_bitcast_fusion) | data formatting | bytes 33554432
  176.1 0.0 reduce-scatter.4.cloned.1.call-update
  176.1 666.1 %reduce-scatter.4.cloned.1.call-done = f32[16,2048]{1,0:T(8,128)} async-done(((f32[2048,2048]{1,0:T(8,128)}), f32[16,2048]{1,0:T(8,128)}) %reduce-scatter.4.cloned.1.call-update) | async-done | bytes 131088 | tf_op jit(solution)/shard_map/reduce_scatter | solution.py:40
  (9 shorter events, 0.1 us)
Async XLA Ops:
  6.5 76.4 %copy-start = (bf16[1,128,2048]{2,1,0:T(8,128)(2,1)S(1)}, bf16[1,128,2048]{2,1,0:T(8,128)(2,1)}, u32[]{:S(2)}) copy-start(bf16[1,128,2048]{2,1,0:T(8,128)(2,1)} %param.7) | copy-start | bytes 1572868
  6.5 81.3 %copy-start.1 = (f32[1,128,2048]{2,1,0:T(8,128)S(1)}, f32[1,128,2048]{2,1,0:T(8,128)}, u32[]{:S(2)}) copy-start(f32[1,128,2048]{2,1,0:T(8,128)} %param.10) | copy-start | bytes 3145732
  6.5 76.4 %all-gather.2.cloned.1.call-start = ((), (), s32[]{:S(2)}) async-start(), calls=%async_computation.1 | async-start | bytes 8454144 | tf_op jit(solution)/shard_map/all_gather | solution.py:27
  7.3 834.9 %reduce-scatter.4.cloned.1.call-start = ((), (), s32[]{:S(2)}) async-start(), calls=%async_computation.2 | async-start | bytes 16908288 | tf_op jit(solution)/shard_map/reduce_scatter | solution.py:40
  7.3 80.5 %collective-permute-start.1 = (f32[1,2048]{1,0:T(1,128)S(1)}, f32[1,2048]{1,0:T(1,128)S(1)}, u32[]{:S(2)}, u32[]{:S(2)}) collective-permute-start(f32[1,2048]{1,0:T(1,128)S(1)} %broadcast.12), channel_id=1, source_target_pairs={{0,1},{1,2},{2,3},{3,4},{4,5},{5,6},{6,7},{8,9},{9,10},{10,11},{11... | collective-permute-start | bytes 24584 | tf_op jit(solution)/shard_map/ppermute | solution.py:16
  8.6 79.2 %collective-permute-start = (f32[1,2048]{1,0:T(1,128)S(1)}, f32[1,2048]{1,0:T(1,128)S(1)}, u32[]{:S(2)}, u32[]{:S(2)}) collective-permute-start(f32[1,2048]{1,0:T(1,128)S(1)} %broadcast.12), channel_id=1, source_target_pairs={{1,0},{2,1},{3,2},{4,3},{5,4},{6,5},{7,6},{9,8},{10,9},{11,10},{12... | collective-permute-start | bytes 24584 | tf_op jit(solution)/shard_map/ppermute | solution.py:17
  83.0 4.9 slice-start
  83.0 5.8 slice-start.1
  90.2 4.3 collective-permute-start.2
  91.5 3.8 collective-permute-start.3
  97.0 5.3 collective-permute-start.4
  98.3 4.8 collective-permute-start.5
  104.7 6.1 collective-permute-start.6
  106.0 5.6 collective-permute-start.7
  113.2 6.1 collective-permute-start.8
  114.5 5.6 collective-permute-start.9
  121.8 6.2 collective-permute-start.10
  123.1 14.3 %copy-start.2 = (f32[1,128,2048]{2,1,0:T(8,128)S(1)}, f32[1,128,2048]{2,1,0:T(8,128)}, u32[]{:S(2)}) copy-start(f32[1,128,2048]{2,1,0:T(8,128)} %param.10) | copy-start | bytes 3145732
  123.1 5.7 collective-permute-start.11
  130.4 6.3 collective-permute-start.12
  131.7 5.6 collective-permute-start.13
  139.0 6.1 collective-permute-start.14
  140.3 5.6 collective-permute-start.15
Sparse Core Ops, SparseCore 0:
  10.3 72.5 all-gather.1
  176.3 665.9 reduce-scatter.3
where the time goes:
time: 850 us; the launch traced here: 849 us
  waiting for transfers between devices  745 us (88%)
  starting transfers between devices  42.9 us (5%)
  matrix products  28.4 us (3%)
  local copies, waits for them, and re-layouts  18.7 us (2%)
  between operations  14.4 us (2%)
    reduce_scatter x1, waiting for transfers between devices, shards(): lax.psum_scatter(lax.dot_general(columns, partial_img, (((0,), (0,)), (()...  666 us
    all_gather x1, waiting for transfers between devices, shards(): lax.all_gather(fine_model, ('freq', 'slab'), axis=0, tiled=True)  72.4 us
    ppermute x8, starting transfers between devices, with_halo(): before = lax.ppermute(last, axis, up)  32.5 us
    unnamed x11, local copies, waits for them, and re-layouts  18.6 us
  transfers between devices with their start and end apart: 18, of which 9 were waited for; matrix products, arithmetic and copies ran while one was open for 1% of the time, Pallas kernels for 0%

commit v1 on v0

--- a/solution.py
+++ b/solution.py
@@ -24,7 +24,12 @@
     columns = oper
     coarse = jnp.dot(
         columns,
-        lax.all_gather(fine_model, ("freq", "slab"), axis=0, tiled=True),
+        jnp.concatenate(
+            lax.all_to_all(
+                jnp.stack([fine_model] * lax.axis_size(("freq", "slab"))), ("freq", "slab"), 0, 0
+            ),
+            axis=0,
+        ),
         preferred_element_type=jnp.float32,
     )
     diag = 4.0 + shift[0] * coarse * coarse

time: 850 us -> 901 us (1.060)
  waiting for transfers between devices: 745 us -> 775 us
  starting transfers between devices: 42.9 us -> 55.5 us
    all_to_all x0 -> x1, waiting for transfers between devices: none -> 98.9 us  [shards(): lax.all_to_all(jnp.stack([fine_model] * lax.axis_size(('freq', 'slab'))),...]
    all_gather x1 -> x0, waiting for transfers between devices: 72.4 us -> none  [shards(): lax.all_gather(fine_model, ('freq', 'slab'), axis=0, tiled=True)]
    all_to_all x0 -> x1, starting transfers between devices: none -> 11.7 us  [shards(): lax.all_to_all(jnp.stack([fine_model] * lax.axis_size(('freq', 'slab'))),...]
where the time goes in v1:
time: 901 us; the launch traced here: 900 us
  waiting for transfers between devices  775 us (86%)
  starting transfers between devices  55.5 us (6%)
  matrix products  32.1 us (4%)
  local copies, waits for them, and re-layouts  23 us (3%)
  between operations  14.4 us (2%)
    reduce_scatter x1, waiting for transfers between devices, shards(): lax.psum_scatter(lax.dot_general(columns, partial_img, (((0,), (0,)), (()...  671 us
    all_to_all x1, waiting for transfers between devices, shards(): lax.all_to_all(jnp.stack([fine_model] * lax.axis_size(('freq', 'slab'))),...  98.9 us
    ppermute x8, starting transfers between devices, with_halo(): before = lax.ppermute(last, axis, up)  33.5 us
  transfers between devices with their start and end apart: 18, of which 9 were waited for; matrix products, arithmetic and copies ran while one was open for 1% of the time, Pallas kernels for 0%

profile of v1, /device:TPU:0, one launch (start us, length us, event | category | flops | bytes accessed | tf_op | source)
XLA Modules:
  0.0 900.2 jit_solution(5276830409550822209)
XLA Ops:
  6.5 0.0 copy-start
  6.5 5.2 stack.2
  11.7 11.7 %all-to-all-start = ((bf16[128,16,2048]{2,1,0:T(8,128)(2,1)}), bf16[128,16,2048]{2,1,0:T(8,128)(2,1)}, u32[]{:S(2)}, u32[]{:S(2)}) async-start(bf16[128,16,2048]{2,1,0:T(8,128)(2,1)} %stack.2), calls=%async_computation | async-start | bytes 16777216 | tf_op jit(solution)/shard_map/all_to_all | solution.py:28
  23.4 0.0 copy-start.1
  23.4 0.0 reduce-scatter.4.cloned.1.call-start
  23.5 1.4 collective-permute-start.1
  24.9 1.3 collective-permute-start
  26.9 98.9 %all-to-all-done = bf16[128,16,2048]{2,1,0:T(8,128)(2,1)} async-done(((bf16[128,16,2048]{2,1,0:T(8,128)(2,1)}), bf16[128,16,2048]{2,1,0:T(8,128)(2,1)}, u32[]{:S(2)}, u32[]{:S(2)}) %all-to-all-start) | async-done | bytes 8388640 | tf_op jit(solution)/shard_map/all_to_all | solution.py:28
  125.8 0.0 copy-done
  125.8 0.0 slice-start
  125.8 4.8 fusion.5
  130.6 0.0 slice-start.1
  130.6 0.0 collective-permute-done.1
  130.6 0.0 collective-permute-done
  130.6 0.0 copy-done.1
  130.6 4.9 fusion.4
  135.5 1.3 collective-permute-start.2
  136.8 3.0 collective-permute-start.3
  139.9 0.0 collective-permute-done.2
  139.9 0.8 collective-permute-done.3
  140.7 0.0 slice-done
  140.7 0.0 slice-done.1
  140.7 1.6 fusion.41
  142.3 1.3 collective-permute-start.4
  143.6 4.8 collective-permute-start.5
  148.4 0.0 collective-permute-done.4
  148.5 0.8 collective-permute-done.5
  149.3 1.6 fusion.36
  150.9 1.3 collective-permute-start.6
  152.2 4.8 collective-permute-start.7
  157.0 0.0 collective-permute-done.6
  157.0 0.8 collective-permute-done.7
  157.8 1.6 fusion.31
  159.4 1.3 collective-permute-start.8
  160.7 4.8 collective-permute-start.9
  165.5 0.0 collective-permute-done.8
  165.5 0.8 collective-permute-done.9
  166.3 1.6 fusion.26
  168.0 1.3 collective-permute-start.10
  169.3 0.0 copy-start.2
  169.3 5.1 collective-permute-start.11
  174.4 0.0 collective-permute-done.10
  174.4 0.6 collective-permute-done.11
  175.0 1.6 fusion.21
  176.6 1.3 collective-permute-start.12
  177.9 4.8 collective-permute-start.13
  182.7 0.0 collective-permute-done.12
  182.7 0.8 collective-permute-done.13
  183.5 0.0 copy-done.2
  183.5 1.6 fusion.16
  185.2 1.3 collective-permute-start.14
  186.5 4.8 collective-permute-start.15
  191.2 0.0 collective-permute-done.14
  191.3 0.8 collective-permute-done.15
  192.1 12.8 %convolution_bitcast_fusion = f32[2048,2048]{0,1:T(8,128)} fusion(f32[1,128,2048]{2,1,0:T(8,128)} %param.11, f32[128,2048]{1,0:T(8,128)S(1)} %fusion.5, f32[128,2048]{1,0:T(8,128)S(1)} %fusion.16, f32[1,2048]{1,0:T(1,128)S(1)} %collective-permute-done.15, f32[1,2048]{1,0:T(1,128)S(1)} %collective-permute-done.14, f32[1,128,2048]{2,1,0:T(8,128)} %param.10, ...), kind=kOutput, calls=%fused_computation | convolution fusion | flops 2150105088 | bytes 29900800 | tf_op jit(solution)/shard_map/dot_general | solution.py:46
  204.9 17.6 %copy.9 = f32[2048,2048]{1,0:T(8,128)} copy(f32[2048,2048]{0,1:T(8,128)} %convolution_bitcast_fusion) | data formatting | bytes 33554432
  222.5 0.0 reduce-scatter.4.cloned.1.call-update
  222.5 670.8 %reduce-scatter.4.cloned.1.call-done = f32[16,2048]{1,0:T(8,128)} async-done(((f32[2048,2048]{1,0:T(8,128)}), f32[16,2048]{1,0:T(8,128)}) %reduce-scatter.4.cloned.1.call-update) | async-done | bytes 131088 | tf_op jit(solution)/shard_map/reduce_scatter | solution.py:45
  (9 shorter events, 0.1 us)
Async XLA Ops:
  6.5 119.2 %copy-start = (bf16[1,128,2048]{2,1,0:T(8,128)(2,1)S(1)}, bf16[1,128,2048]{2,1,0:T(8,128)(2,1)}, u32[]{:S(2)}) copy-start(bf16[1,128,2048]{2,1,0:T(8,128)(2,1)} %param.7) | copy-start | bytes 1572868
  11.7 114.0 %all-to-all-start = ((bf16[128,16,2048]{2,1,0:T(8,128)(2,1)}), bf16[128,16,2048]{2,1,0:T(8,128)(2,1)}, u32[]{:S(2)}, u32[]{:S(2)}) async-start(bf16[128,16,2048]{2,1,0:T(8,128)(2,1)} %stack.2), calls=%async_computation | async-start | bytes 16777216 | tf_op jit(solution)/shard_map/all_to_all | solution.py:28
  23.4 107.2 %copy-start.1 = (f32[1,128,2048]{2,1,0:T(8,128)S(1)}, f32[1,128,2048]{2,1,0:T(8,128)}, u32[]{:S(2)}) copy-start(f32[1,128,2048]{2,1,0:T(8,128)} %param.10) | copy-start | bytes 3145732
  23.4 869.9 %reduce-scatter.4.cloned.1.call-start = ((), (), s32[]{:S(2)}) async-start(), calls=%async_computation.2 | async-start | bytes 16908288 | tf_op jit(solution)/shard_map/reduce_scatter | solution.py:45
  23.5 107.1 %collective-permute-start.1 = (f32[1,2048]{1,0:T(1,128)S(1)}, f32[1,2048]{1,0:T(1,128)S(1)}, u32[]{:S(2)}, u32[]{:S(2)}) collective-permute-start(f32[1,2048]{1,0:T(1,128)S(1)} %broadcast.14), channel_id=1, source_target_pairs={{0,1},{1,2},{2,3},{3,4},{4,5},{5,6},{6,7},{8,9},{9,10},{10,11},{11... | collective-permute-start | bytes 24584 | tf_op jit(solution)/shard_map/ppermute | solution.py:16
  24.9 105.7 %collective-permute-start = (f32[1,2048]{1,0:T(1,128)S(1)}, f32[1,2048]{1,0:T(1,128)S(1)}, u32[]{:S(2)}, u32[]{:S(2)}) collective-permute-start(f32[1,2048]{1,0:T(1,128)S(1)} %broadcast.14), channel_id=1, source_target_pairs={{1,0},{2,1},{3,2},{4,3},{5,4},{6,5},{7,6},{9,8},{10,9},{11,10},{12... | collective-permute-start | bytes 24584 | tf_op jit(solution)/shard_map/ppermute | solution.py:17
  125.8 14.9 %slice-start = ((s8[8388608]{0:T(1024)(128)(4,1)}), s8[4194304]{0:T(1024)(128)(4,1)S(1)}, s32[]{:S(2)}) async-start(s8[8388608]{0:T(1024)(128)(4,1)} %bitcast.39), calls=%async_computation.3 | async-start | bytes 8388608
  130.6 10.1 %slice-start.1 = ((s8[8388608]{0:T(1024)(128)(4,1)}), s8[4194304]{0:T(1024)(128)(4,1)S(1)}, s32[]{:S(2)}) async-start(s8[8388608]{0:T(1024)(128)(4,1)} %bitcast.39), calls=%async_computation.4 | async-start | bytes 8388608
  135.5 4.3 collective-permute-start.2
  136.8 3.8 collective-permute-start.3
  142.3 6.1 collective-permute-start.4
  143.6 5.6 collective-permute-start.5
  150.9 6.1 collective-permute-start.6
  152.2 5.6 collective-permute-start.7
  159.4 6.1 collective-permute-start.8
  160.7 5.6 collective-permute-start.9
  168.0 6.4 collective-permute-start.10
  169.3 14.3 %copy-start.2 = (f32[1,128,2048]{2,1,0:T(8,128)S(1)}, f32[1,128,2048]{2,1,0:T(8,128)}, u32[]{:S(2)}) copy-start(f32[1,128,2048]{2,1,0:T(8,128)} %param.10) | copy-start | bytes 3145732
  169.3 5.7 collective-permute-start.11
  176.6 6.1 collective-permute-start.12
  177.9 5.6 collective-permute-start.13
  185.2 6.1 collective-permute-start.14
  186.5 5.6 collective-permute-start.15
Sparse Core Ops, SparseCore 0:
  222.6 670.6 reduce-scatter.3
